TPU v7x, 32 devices: a whole 2x2x4 slice. The times are simulated.
32 devices in a mesh: gx: 4 (over y, core), gy: 8 (over z, x).
Axes of the slice: x: 2, y: 2, z: 4, core: 2. Of those that a mesh axis runs over, the one named last changes fastest.
Arguments:
- row_ids: int32 [65536], P(('gx', 'gy')), may hold values from 0 to 262143, as said below
- block_map: int32 [2048], replicated, may hold values from 0 to 2047, as said below
- grad_tiles: float32 [65536, 128], P(('gx', 'gy')), may hold values from -6 to 6
- table: float32 [262144, 128], P(('gx', 'gy')), may hold values from -4 to 4
- accum: float32 [262144], P(('gx', 'gy')), may hold values from 0.05 to 2
Outputs:
- new_table: float32 [262144, 128], P(('gx', 'gy'))
- new_accum: float32 [262144], P(('gx', 'gy'))
Inputs may be any that keep to these rules, and one draw needn't show every extreme that they name: `row_ids`: storage position p lies on device p // 8192 of the gx+gy order. Among the lookups of one device, at most 128 have positions on any one device; in every draw one device holds exactly 128 positions of the lookups of every device. Rows repeat within and across devices. `block_map`: each number appears once.
All inputs are finite; a program needn't handle non-finite values.
Results may differ from a plain program's by a relative error of at most 0.00002.
Values sent between devices are 32-bit elements; how exact they have to be, the bound alone decides.
No kernel may reach another device: no remote copies, remote signals or barrier semaphores. Data moves between devices by JAX's collectives and lax.ppermute only.
A program may use at most 64 MiB of HBM per device.

v0:
```python
import jax
import jax.numpy as jnp
from jax import lax
from jax.sharding import PartitionSpec as P

BLOCK = 128


learning_rate = 0.25
epsilon = 1e-08


def on_device(row_ids, block_map, grad_tiles, table, accum):
    gx_count = lax.axis_size("gx")
    gy_count = lax.axis_size("gy")
    devices = gx_count * gy_count
    rows_dev = table.shape[0]
    look_count = row_ids.shape[0]
    feature_count = grad_tiles.shape[1]
    capacity = 2 * look_count // devices
    position = jnp.take(block_map, row_ids // BLOCK) * BLOCK + row_ids % BLOCK
    owner = position // rows_dev
    slot_ids = position % rows_dev
    owner_hot = (owner[:, None] == jnp.arange(devices, dtype=jnp.int32)[None, :]).astype(jnp.int32)
    running = jnp.cumsum(owner_hot, axis=0) - owner_hot
    rank = jnp.sum(running * owner_hot, axis=1)
    target = owner * capacity + rank
    send_rows = (
        jnp.zeros((devices * capacity, feature_count), jnp.float32).at[target].set(grad_tiles)
    )
    send_slots = jnp.full((devices * capacity,), rows_dev, jnp.int32).at[target].set(slot_ids)
    arrived_rows, arrived_slots = (
        lax.all_to_all(send_rows, ("gx", "gy"), split_axis=0, concat_axis=0, tiled=True),
        lax.all_to_all(send_slots, ("gx", "gy"), split_axis=0, concat_axis=0, tiled=True),
    )
    row_grad = (
        jnp.zeros((rows_dev, feature_count), jnp.float32)
        .at[arrived_slots]
        .add(arrived_rows, mode="drop")
    )
    new_accum = accum + jnp.mean(row_grad * row_grad, axis=1)
    new_table = table - learning_rate * row_grad / (jnp.sqrt(new_accum) + epsilon)[:, None]
    return (new_table, new_accum)


def solution(mesh):
    in_specs = (P(("gx", "gy")), P(), P(("gx", "gy"), None), P(("gx", "gy"), None), P(("gx", "gy")))
    out_specs = (P(("gx", "gy"), None), P(("gx", "gy")))
    return jax.shard_map(
        on_device, mesh=mesh, in_specs=in_specs, out_specs=out_specs, check_vma=False
    )
```

profile of v0, /device:TPU:0, one launch (start us, length us, event | category | flops | bytes accessed | tf_op | source)
XLA Modules:
  0.0 135.2 jit_solution(1383733932680038819)
XLA Ops:
  0.6 0.0 copy-start
  0.6 0.7 broadcast_clamp_fusion
  1.4 0.0 copy-done
  1.4 0.0 copy-start.2
  1.4 11.8 %gather_fusion = s32[2048]{0:T(1024)S(1)} fusion(s32[2048]{0:T(1024)S(1)} %copy-done, s32[2048]{0:T(1024)S(1)} %broadcast_clamp_fusion), kind=kCustom, calls=%fused_computation | custom fusion | bytes 24576 | tf_op jit(solution)/shard_map/jit(_take)/gather | solution.py:21
  13.2 0.0 copy-done.2
  13.3 9.1 %reduce-window.6 = s32[32,16,128]{2,1,0:T(8,128)S(1)} reduce-window(s32[32,16,128]{2,1,0:T(8,128)S(1)} %fusion.7, s32[]{:T(128)} %constant.71.clone.1), window={size=1x1x128 pad=0_0x0_0x127_0}, to_apply=%region_0.1 | reduce-window | flops 8323072 | bytes 524292 | tf_op jit(solution)/shard_map/reduce-window
  22.4 0.1 slice.10
  22.5 0.2 copy.12
  22.7 0.2 reduce-window.9
  22.9 0.1 broadcast_add_fusion
  23.1 0.1 fusion.6
  23.2 8.6 %scatter_custom_fusion = s32[4096]{0:T(1024)} fusion(s32[2048]{0:T(1024)S(1)} %compare_select_fusion.1, s32[2048]{0:T(1024)S(1)} %get-tuple-element.4, s32[]{:T(128)} %constant.69.clone.1), kind=kCustom, calls=%fused_computation.36 | custom fusion | bytes 16388 | tf_op jit(solution)/shard_map/scatter | solution.py:31
  31.8 7.3 %all-to-all-start = ((s32[32,128,1]{1,2,0:T(1,128)}), s32[32,128,1]{1,2,0:T(1,128)S(1)}, u32[]{:S(2)}, u32[]{:S(2)}) async-start(s32[32,128,1]{1,2,0:T(1,128)} %bitcast.5), calls=%async_computation | async-start | bytes 32768 | tf_op jit(solution)/shard_map/all_to_all | solution.py:34
  39.2 7.4 %scatter_custom_fusion.1 = f32[4096,128]{1,0:T(8,128)} fusion(s32[2048]{0:T(1024)S(1)} %compare_select_fusion.1, f32[2048,128]{1,0:T(8,128)} %param.7, f32[]{:T(128)} %constant.68.clone.1), kind=kCustom, calls=%fused_computation.8 | custom fusion | bytes 2097664 | tf_op jit(solution)/shard_map/scatter | solution.py:29
  46.5 0.0 all-to-all-done
  46.5 5.8 %all-to-all-start.1 = ((f32[32,128,128]{2,1,0:T(8,128)}), f32[32,128,128]{2,1,0:T(8,128)S(1)}, u32[]{:S(2)}, u32[]{:S(2)}) async-start(f32[32,128,128]{2,1,0:T(8,128)} %bitcast.8), calls=%async_computation.1 | async-start | bytes 4194304 | tf_op jit(solution)/shard_map/all_to_all | solution.py:33
  52.4 49.9 %all-to-all-done.1 = f32[32,128,128]{2,1,0:T(8,128)S(1)} async-done(((f32[32,128,128]{2,1,0:T(8,128)}), f32[32,128,128]{2,1,0:T(8,128)S(1)}, u32[]{:S(2)}, u32[]{:S(2)}) %all-to-all-start.1) | async-done | bytes 2097184 | tf_op jit(solution)/shard_map/all_to_all | solution.py:33
  102.3 24.6 %scatter_custom_fusion.2 = f32[8192,128]{1,0:T(8,128)} fusion(s32[4096]{0:T(1024)S(1)} %bitcast.36, f32[4096,128]{1,0:T(8,128)S(1)} %bitcast.32, f32[]{:T(128)} %constant.68.clone.1), kind=kCustom, calls=%fused_computation.6 | custom fusion | flops 524288 | bytes 4194308 | tf_op jit(solution)/shard_map/scatter-add | solution.py:39
  126.9 3.5 %multiply_reduce_fusion = f32[8192]{0:T(1024)S(1)} fusion(f32[8192,128]{1,0:T(8,128)} %scatter_custom_fusion.2), kind=kLoop, calls=%fused_computation.5 | loop fusion | flops 2088960 | bytes 4227072 | tf_op jit(solution)/shard_map/reduce_sum | solution.py:41
  130.4 0.0 copy-done.3
  130.4 0.6 sqrt_add_fusion
  131.0 0.0 copy-done.1
  131.0 4.2 %divide_subtract_fusion = f32[8192,128]{1,0:T(8,128)} fusion(f32[8192,128]{1,0:T(8,128)} %param.8, f32[8192,128]{1,0:T(8,128)S(1)} %copy-done.1, f32[8192]{0:T(1024)S(1)} %get-tuple-element.2), kind=kLoop, calls=%fused_computation.4 | loop fusion | flops 3145728 | bytes 12615680 | tf_op jit(solution)/shard_map/sub | solution.py:42
  (8 shorter events, 0.1 us)
Async XLA Ops:
  0.6 0.7 copy-start
  1.4 11.8 %copy-start.2 = (s32[2048]{0:T(1024)S(1)}, s32[2048]{0:T(1024)}, u32[]{:S(2)}) copy-start(s32[2048]{0:T(1024)} %param.5) | copy-start | bytes 24580
  31.8 14.7 %all-to-all-start = ((s32[32,128,1]{1,2,0:T(1,128)}), s32[32,128,1]{1,2,0:T(1,128)S(1)}, u32[]{:S(2)}, u32[]{:S(2)}) async-start(s32[32,128,1]{1,2,0:T(1,128)} %bitcast.5), calls=%async_computation | async-start | bytes 32768 | tf_op jit(solution)/shard_map/all_to_all | solution.py:34
  46.5 55.8 %all-to-all-start.1 = ((f32[32,128,128]{2,1,0:T(8,128)}), f32[32,128,128]{2,1,0:T(8,128)S(1)}, u32[]{:S(2)}, u32[]{:S(2)}) async-start(f32[32,128,128]{2,1,0:T(8,128)} %bitcast.8), calls=%async_computation.1 | async-start | bytes 4194304 | tf_op jit(solution)/shard_map/all_to_all | solution.py:33
  102.3 28.1 %copy-start.3 = (f32[8192]{0:T(1024)S(1)}, f32[8192]{0:T(1024)}, u32[]{:S(2)}) copy-start(f32[8192]{0:T(1024)} %param.9) | copy-start | bytes 98308
  126.9 4.1 %copy-start.1 = (f32[8192,128]{1,0:T(8,128)S(1)}, f32[8192,128]{1,0:T(8,128)}, u32[]{:S(2)}) copy-start(f32[8192,128]{1,0:T(8,128)} %scatter_custom_fusion.2) | copy-start | bytes 12582916
where the time goes:
time: 136 us; the launch traced here: 135 us
  waiting for transfers between devices  49.9 us (37%)
  other arithmetic  43.2 us (32%)
  local copies, waits for them, and re-layouts  28.2 us (21%)
  starting transfers between devices  13.2 us (10%)
    all_to_all x1, waiting for transfers between devices, on_device(): lax.all_to_all(send_rows, ('gx', 'gy'), split_axis=0, concat_axis=0, tile...  49.9 us
    scatter-add x1, other arithmetic, on_device(): row_grad = jnp.zeros((rows_dev, feature_count), jnp.float32).at[arrived_s...  24.6 us
    gather x1, local copies, waits for them, and re-layouts, on_device(): position = jnp.take(block_map, row_ids // BLOCK) * BLOCK + row_ids % BLOCK  11.8 us
    another operation x3, other arithmetic  9.41 us
    scatter x1, local copies, waits for them, and re-layouts, on_device(): jnp.full((devices * capacity,), rows_dev, jnp.int32).at[target]  8.62 us
    scatter x1, local copies, waits for them, and re-layouts, on_device(): jnp.zeros((devices * capacity, feature_count), jnp.float32).at[target]  7.36 us
    all_to_all x1, starting transfers between devices, on_device(): lax.all_to_all(send_slots, ('gx', 'gy'), split_axis=0, concat_axis=0, til...  7.33 us
    all_to_all x1, starting transfers between devices, on_device(): lax.all_to_all(send_rows, ('gx', 'gy'), split_axis=0, concat_axis=0, tile...  5.83 us
  transfers between devices with their start and end apart: 2, of which 1 were waited for; matrix products, arithmetic and copies ran while one was open for 5% of the time, Pallas kernels for 0%

commit v1 on v0

v1 whole, which is shorter than its diff:
```python
import functools

import jax
import jax.numpy as jnp
from jax import lax
from jax.experimental import pallas as pl
from jax.experimental.pallas import tpu as pltpu
from jax.sharding import PartitionSpec as P

BLOCK = 128
LANES = 128
STREAMS = 4
UNROLL = 16
CHUNKS = 8

learning_rate = 0.25
epsilon = 1e-08


def split(x, n):
    if n & (n - 1) == 0:
        return lax.shift_right_logical(x, n.bit_length() - 1), x & (n - 1)
    return lax.div(x, n), lax.rem(x, n)


def bin_kernel(
    devices, rows_dev, ids_ref, map_ref, grad_hbm, send_ref, info_ref, grad_ref, cols, marks, target_vmem, target, sums, sems
):
    blocks = ids_ref.shape[0]
    width = send_ref.shape[0] // devices
    slots = width - 1
    drop = devices * width
    fetch = pltpu.make_async_copy(grad_hbm, grad_ref, sems.at[0])
    fetch.start()

    block, within = split(ids_ref[...], BLOCK)
    high, low = split(block, LANES)
    mapped = jnp.zeros_like(block)
    for h in range(map_ref.shape[0]):
        row = jnp.broadcast_to(map_ref[h : h + 1, :], low.shape)
        mapped = jnp.where(high == h, jnp.take_along_axis(row, low, axis=1), mapped)
    position = mapped * BLOCK + within
    owner, slot = split(position, rows_dev)

    def column(row):
        return jnp.transpose(jnp.broadcast_to(row, (LANES, LANES)))

    for b in range(blocks):
        cols[b * LANES : (b + 1) * LANES, :] = column(position[b : b + 1, :])
    rows = [jnp.broadcast_to(position[b : b + 1, :], (8, LANES)) for b in range(blocks)]
    per_block = LANES // 8
    none = blocks * per_block
    first = [jnp.full((8, LANES), none, jnp.int32) for _ in range(blocks)]
    for v in reversed(range(blocks * per_block)):
        col = cols[8 * v : 8 * v + 8, :]
        for b in range(v // per_block, blocks):
            first[b] = jnp.where(col == rows[b], v, first[b])
    sublane = lax.broadcasted_iota(jnp.int32, (8, LANES), 0)
    lane = lax.broadcasted_iota(jnp.int32, (1, LANES), 1)
    leads = [
        jnp.min(first[b] * 8 + sublane, axis=0, keepdims=True) == lane + b * LANES for b in range(blocks)
    ]

    device = lax.broadcasted_iota(jnp.int32, (devices, LANES), 0)
    owned = [device == owner[b : b + 1, :] for b in range(blocks)]
    hot = [owned[b] & leads[b] for b in range(blocks)]
    hot16 = jnp.concatenate([h.astype(jnp.float32) for h in hot], axis=0).astype(jnp.bfloat16)
    i0 = lax.broadcasted_iota(jnp.int32, (LANES, 2 * LANES), 0)
    i1 = lax.broadcasted_iota(jnp.int32, (LANES, 2 * LANES), 1)
    ahead = ((i0 < i1)).astype(jnp.float32).astype(jnp.bfloat16)
    counted = jnp.dot(hot16, ahead, preferred_element_type=jnp.float32)
    counts = jnp.zeros((devices, LANES), jnp.float32)
    header_high = jnp.zeros((devices, LANES), jnp.float32)
    header_low = jnp.zeros((devices, LANES), jnp.float32)
    slot_high, slot_low = split(slot, LANES)
    lanes = lax.broadcasted_iota(jnp.int32, (LANES, LANES), 1)
    for b in range(blocks):
        here = counted[b * devices : (b + 1) * devices]
        rank = jnp.sum(jnp.where(owned[b], here[:, :LANES] + counts, 0.0), axis=0, keepdims=True)
        counts = counts + here[:, LANES:]
        rank_col = column(rank.astype(jnp.int32))
        marks[b * LANES : (b + 1) * LANES, :] = rank_col
        place = (rank_col == lanes).astype(jnp.float32).astype(jnp.bfloat16)
        both = jnp.concatenate(
            [
                jnp.where(hot[b], slot_high[b : b + 1, :].astype(jnp.float32), 0.0),
                jnp.where(hot[b], slot_low[b : b + 1, :].astype(jnp.float32), 0.0),
            ],
            axis=0,
        ).astype(jnp.bfloat16)
        parts = jnp.dot(both, place, preferred_element_type=jnp.float32)
        header_high = header_high + parts[:devices]
        header_low = header_low + parts[devices:]

    ranks = [jnp.full((8, LANES), drop, jnp.int32) for _ in range(blocks)]
    for v in reversed(range(blocks * per_block)):
        col = cols[8 * v : 8 * v + 8, :]
        mark = marks[8 * v : 8 * v + 8, :]
        for b in range(v // per_block, blocks):
            ranks[b] = jnp.where(col == rows[b], mark, ranks[b])
    rank = jnp.concatenate([jnp.min(r, axis=0, keepdims=True) for r in ranks], axis=0)
    target_vmem[...] = jnp.where(rank < slots, owner * width + rank, drop)
    send_target = pltpu.make_async_copy(target_vmem, target, sems.at[1])
    send_target.start()
    info_ref[0:blocks, :] = rank
    info_ref[blocks : 2 * blocks, :] = position

    for s in range(STREAMS):
        sums[s][...] = jnp.zeros_like(sums[s])
    over = jnp.max(counts) > slots
    header = jnp.where(
        lane.astype(jnp.float32) < jnp.minimum(counts, slots), header_high * LANES + header_low, float(rows_dev)
    )
    header = jnp.where(lane == LANES - 1, jnp.minimum(counts, slots), header)
    header = jnp.where(lane == LANES - 2, jnp.where(over, 1.0, 0.0), header)
    send_target.wait()
    fetch.wait()

    @pl.loop(0, blocks)
    def _(b):
        @pl.loop(0, LANES // UNROLL)
        def _(q):
            c0 = q * UNROLL
            at = [target[b, c0 + u] for u in range(UNROLL)]
            for g in range(0, UNROLL, STREAMS):
                old = [sums[s][pl.ds(at[g + s], 1), :] for s in range(STREAMS)]
                new = [
                    old[s] + grad_ref[pl.ds(b * LANES + c0 + g + s, 1), :] for s in range(STREAMS)
                ]
                for s in range(STREAMS):
                    sums[s][pl.ds(at[g + s], 1), :] = new[s]

    total = sums[0][0:drop, :]
    for s in range(1, STREAMS):
        total = total + sums[s][0:drop, :]
    send_ref[...] = total
    send_ref[pl.ds(slots, devices, stride=width), :] = header


def update_kernel(
    devices, got_ref, more_head_ref, more_hbm, accum_ref, table_hbm, table_out, accum_out,
    sums, table, more, head_vmem, head, sems_in, sems_out, sem,
):
    width = got_ref.shape[0] // devices
    slots = width - 1
    more_width = more_hbm.shape[0] // devices
    rows_dev = table.shape[0]
    chunk = rows_dev // CHUNKS
    unroll = UNROLL if width % UNROLL == 0 else 8
    head_vmem[0:devices, :] = got_ref[pl.ds(slots, devices, stride=width), :].astype(jnp.int32)
    head_vmem[devices : 2 * devices, :] = more_head_ref[...]
    load_head = pltpu.make_async_copy(head_vmem, head, sem)
    load_head.start()
    loads = [
        pltpu.make_async_copy(
            table_hbm.at[pl.ds(c * chunk, chunk), :], table.at[pl.ds(c * chunk, chunk), :], sems_in.at[c]
        )
        for c in range(CHUNKS)
    ]
    for load in loads:
        load.start()
    sums[...] = jnp.zeros_like(sums)
    load_head.wait()

    def add_rows(source_head, rows_ref, base, count):
        @pl.loop(0, lax.div(count + unroll - 1, unroll))
        def _(q):
            r0 = q * unroll
            at = [head[source_head, r0 + u] for u in range(unroll)]
            old = [sums[pl.ds(a, 1), :] for a in at]
            new = [old[u] + rows_ref[pl.ds(base + r0 + u, 1), :] for u in range(unroll)]
            for u in range(unroll):
                sums[pl.ds(at[u], 1), :] = new[u]

    @pl.loop(0, devices)
    def _(d):
        add_rows(d, got_ref, d * width, head[d, LANES - 1])

    @pl.loop(0, devices)
    def _(d):
        @pl.when(head[devices + d, LANES - 1] > 0)
        def _():
            copy = pltpu.make_async_copy(
                more_hbm.at[pl.ds(d * more_width, more_width), :], more.at[pl.ds(0, more_width), :], sem
            )
            copy.start()
            copy.wait()
            add_rows(devices + d, more, 0, head[devices + d, LANES - 1])

    groups = chunk // LANES
    stores = []
    for c in range(CHUNKS):
        loads[c].wait()

        @pl.loop(0, groups)
        def _(i):
            k = c * groups + i
            here = pl.ds(pl.multiple_of(k * LANES, LANES), LANES)
            grad = sums[here, :]
            mean = jnp.sum(jnp.transpose(grad * grad), axis=0, keepdims=True) * (1.0 / LANES)
            new_accum = accum_ref[pl.ds(k, 1), :] + mean
            accum_out[pl.ds(k, 1), :] = new_accum
            scale = learning_rate / (jnp.sqrt(new_accum) + epsilon)
            table[here, :] = table[here, :] - jnp.transpose(jnp.broadcast_to(scale, (LANES, LANES))) * grad

        store = pltpu.make_async_copy(
            table.at[pl.ds(c * chunk, chunk), :], table_out.at[pl.ds(c * chunk, chunk), :], sems_out.at[c]
        )
        store.start()
        stores.append(store)
    for store in stores:
        store.wait()


def on_device(row_ids, block_map, grad_tiles, table, accum):
    axes = ("gx", "gy")
    devices = lax.axis_size("gx") * lax.axis_size("gy")
    rows_dev, features = table.shape
    look_count = row_ids.shape[0]
    capacity = 2 * look_count // devices
    width = -(-capacity * 13 // 16 // 8) * 8
    slots = width - 1
    more_slots = -(-(capacity - slots) // UNROLL) * UNROLL
    blocks = look_count // LANES
    vmem = pl.BlockSpec(memory_space=pltpu.VMEM)
    hbm = pl.BlockSpec(memory_space=pl.ANY)

    send, info = pl.pallas_call(
        functools.partial(bin_kernel, devices, rows_dev),
        out_shape=(
            jax.ShapeDtypeStruct((devices * width, features), jnp.float32),
            jax.ShapeDtypeStruct((2 * blocks, LANES), jnp.int32),
        ),
        in_specs=[vmem, vmem, hbm],
        out_specs=(vmem, vmem),
        scratch_shapes=[
            pltpu.VMEM((look_count, features), jnp.float32),
            pltpu.VMEM((look_count, LANES), jnp.int32),
            pltpu.VMEM((look_count, LANES), jnp.int32),
            pltpu.VMEM((blocks, LANES), jnp.int32),
            pltpu.SMEM((blocks, LANES), jnp.int32),
            [pltpu.VMEM((devices * width + 8, features), jnp.float32)] * STREAMS,
            pltpu.SemaphoreType.DMA((2,)),
        ],
        compiler_params=pltpu.CompilerParams(vmem_limit_bytes=24 << 20),
        name="bin_rows",
    )(row_ids.reshape(blocks, LANES), block_map.reshape(-1, LANES), grad_tiles)

    got = lax.all_to_all(send, axes, split_axis=0, concat_axis=0, tiled=True)

    def second_round(_):
        rank, position = info[:blocks].reshape(-1), info[blocks:].reshape(-1)
        owner, slot = position // rows_dev, position % rows_dev
        limit = devices * more_slots
        at = jnp.where(rank >= slots, owner * more_slots + rank - slots, limit)
        rows = jnp.zeros((limit, features), jnp.float32).at[at].add(grad_tiles, mode="drop")
        places = jnp.full((limit,), rows_dev, jnp.int32).at[at].set(slot, mode="drop")
        rows = lax.all_to_all(rows, axes, split_axis=0, concat_axis=0, tiled=True)
        places = lax.all_to_all(places, axes, split_axis=0, concat_axis=0, tiled=True)
        places = places.reshape(devices, more_slots)
        count = jnp.sum((places < rows_dev).astype(jnp.int32), axis=1, keepdims=True)
        places = jnp.pad(places, ((0, 0), (0, LANES - 1 - more_slots)), constant_values=rows_dev)
        return rows, jnp.concatenate([places, count], axis=1)

    def one_round(_):
        return (
            jnp.zeros((devices * more_slots, features), jnp.float32),
            jnp.zeros((devices, LANES), jnp.int32),
        )

    over = jnp.max(got.reshape(devices, width, features)[:, slots, LANES - 2]) > 0.5
    more, more_head = lax.cond(over, second_round, one_round, None)

    new_table, new_accum = pl.pallas_call(
        functools.partial(update_kernel, devices),
        out_shape=(
            jax.ShapeDtypeStruct(table.shape, jnp.float32),
            jax.ShapeDtypeStruct((rows_dev // LANES, LANES), jnp.float32),
        ),
        in_specs=[vmem, vmem, hbm, vmem, hbm],
        out_specs=(hbm, vmem),
        scratch_shapes=[
            pltpu.VMEM((rows_dev + 8, features), jnp.float32),
            pltpu.VMEM((rows_dev, features), jnp.float32),
            pltpu.VMEM((more_slots + UNROLL, features), jnp.float32),
            pltpu.VMEM((2 * devices, LANES), jnp.int32),
            pltpu.SMEM((2 * devices, LANES), jnp.int32),
            pltpu.SemaphoreType.DMA((CHUNKS,)),
            pltpu.SemaphoreType.DMA((CHUNKS,)),
            pltpu.SemaphoreType.DMA(()),
        ],
        compiler_params=pltpu.CompilerParams(vmem_limit_bytes=24 << 20),
        name="apply_step",
    )(got, more_head, more, accum.reshape(-1, LANES), table)
    return new_table, new_accum.reshape(-1)


def solution(mesh):
    in_specs = (P(("gx", "gy")), P(), P(("gx", "gy"), None), P(("gx", "gy"), None), P(("gx", "gy")))
    out_specs = (P(("gx", "gy"), None), P(("gx", "gy")))
    return jax.shard_map(
        on_device, mesh=mesh, in_specs=in_specs, out_specs=out_specs, check_vma=False
    )
```

time: 136 us -> 88.6 us (0.65)
  other arithmetic: 43.2 us -> 0.7 us
  Pallas kernels: 0 us -> 32.8 us
  local copies, waits for them, and re-layouts: 28.2 us -> 4.42 us
  waiting for transfers between devices: 49.9 us -> 41.5 us
  starting transfers between devices: 13.2 us -> 7.33 us
    pallas_call x0 -> x2, Pallas kernels: none -> 32.8 us  [the longest x1 22.8 us: on_device(): pl.pallas_call(functools.partial(update_kernel, devices), out_shape=(jax....]
    scatter-add x1 -> x0, other arithmetic: 24.6 us -> none  [on_device(): row_grad = jnp.zeros((rows_dev, feature_count), jnp.float32).at[arrived_s...]
    scatter x2 -> x0, local copies, waits for them, and re-layouts: 16 us -> none  [the longest x1 8.62 us: on_device(): jnp.full((devices * capacity,), rows_dev, jnp.int32).at[target]]
    gather x1 -> x0, local copies, waits for them, and re-layouts: 11.8 us -> none  [on_device(): position = jnp.take(block_map, row_ids // BLOCK) * BLOCK + row_ids % BLOCK]
    another operation x3 -> x0, other arithmetic: 9.41 us -> none
    all_to_all x2 -> x1, waiting for transfers between devices: 49.9 us -> 41.5 us  [on_device(): got = lax.all_to_all(send, axes, split_axis=0, concat_axis=0, tiled=True)]
    all_to_all x2 -> x1, starting transfers between devices: 13.2 us -> 7.33 us  [on_device(): got = lax.all_to_all(send, axes, split_axis=0, concat_axis=0, tiled=True)]
    sub x1 -> x0, other arithmetic: 4.22 us -> none  [on_device(): table - learning_rate * row_grad / (jnp.sqrt(new_accum) + epsilon)[:, None]]
  transfers between devices with their start and end apart: 2 -> 1, of which waited for: 1 -> 1; matrix products, arithmetic and copies ran while one was open for 5% -> 0% of each run, Pallas kernels for 0% -> 0%
where the time goes in v1:
time: 88.6 us; the launch traced here: 88.1 us
  waiting for transfers between devices  41.5 us (47%)
  Pallas kernels  32.8 us (37%)
  starting transfers between devices  7.33 us (8%)
  local copies, waits for them, and re-layouts  4.42 us (5%)
  between operations  1.32 us (1%)
    all_to_all x1, waiting for transfers between devices, on_device(): got = lax.all_to_all(send, axes, split_axis=0, concat_axis=0, tiled=True)  41.5 us
    pallas_call x1, Pallas kernels, on_device(): pl.pallas_call(functools.partial(update_kernel, devices), out_shape=(jax....  22.8 us
    pallas_call x1, Pallas kernels, on_device(): pl.pallas_call(functools.partial(bin_kernel, devices, rows_dev), out_shap...  10 us
    all_to_all x1, starting transfers between devices, on_device(): got = lax.all_to_all(send, axes, split_axis=0, concat_axis=0, tiled=True)  7.33 us
    unnamed x8, local copies, waits for them, and re-layouts  3.58 us
  transfers between devices with their start and end apart: 1, of which 1 were waited for; matrix products, arithmetic and copies ran while one was open for 0% of the time, Pallas kernels for 0%

profile of v1, /device:TPU:0, one launch (start us, length us, event | category | flops | bytes accessed | tf_op | source)
XLA Modules:
  0.0 88.1 jit_solution(9339047980257067501)
XLA Ops:
  0.6 0.0 copy-start.2
  0.6 0.7 copy-done.2
  1.3 0.0 copy-start.3
  1.3 0.7 copy-done.3
  2.0 10.0 %bin_rows.1 = (f32[3328,128]{1,0:T(8,128)}, s32[32,128]{1,0:T(8,128)S(1)}) custom-call(s32[16,128]{1,0:T(8,128)S(1)} %bitcast.20, s32[16,128]{1,0:T(8,128)S(1)} %bitcast.21, f32[2048,128]{1,0:T(8,128)} %grad_hbm.1), custom_call_target="tpu_custom_call" | custom-call | tf_op jit(solution)/shard_map/bin_rows/pallas_call | solution.py:228
  12.1 7.3 %all-to-all-start.2 = ((f32[32,104,128]{2,1,0:T(8,128)}), f32[32,104,128]{2,1,0:T(8,128)S(1)}, u32[]{:S(2)}, u32[]{:S(2)}) async-start(f32[32,104,128]{2,1,0:T(8,128)} %bitcast.10), calls=%async_computation.2 | async-start | bytes 3407872 | tf_op jit(solution)/shard_map/all_to_all | solution.py:249
  19.4 0.0 copy-start.1
  19.4 41.5 %all-to-all-done.2 = f32[32,104,128]{2,1,0:T(8,128)S(1)} async-done(((f32[32,104,128]{2,1,0:T(8,128)}), f32[32,104,128]{2,1,0:T(8,128)S(1)}, u32[]{:S(2)}, u32[]{:S(2)}) %all-to-all-start.2) | async-done | bytes 1703968 | tf_op jit(solution)/shard_map/all_to_all | solution.py:249
  60.9 0.7 slice_reduce_fusion
  62.3 0.9 conditional.1
  62.3 0.8 broadcast.114
  63.1 0.0 copy-done.1
  63.1 0.0 copy-start
  63.1 2.2 %copy-done = f32[8192,128]{1,0:T(8,128)S(1)} copy-done((f32[8192,128]{1,0:T(8,128)S(1)}, f32[8192,128]{1,0:T(8,128)}, u32[]{:S(2)}) %copy-start) | copy-done | bytes 4194328
  65.3 22.8 %apply_step.1 = (f32[8192,128]{1,0:T(8,128)}, f32[64,128]{1,0:T(8,128)}) custom-call(f32[3328,128]{1,0:T(8,128)S(1)} %bitcast.18, s32[32,128]{1,0:T(8,128)S(1)} %get-tuple-element.16.more_head_ref, f32[1024,128]{1,0:T(8,128)} %get-tuple-element.17.more_hbm, f32[64,128]{1,0:T(8,128)S(1)} %bitcast.19, f32[8192,128]{1,0:T(8,128)S(1)} %copy-done), custom_call_target="tpu_custom_call" | custom-call | tf_op jit(solution)/shard_map/apply_step/pallas_call | solution.py:274
  (1 shorter events, 0.0 us)
Async XLA Ops:
  0.6 0.7 copy-start.2
  1.3 0.7 copy-start.3
  12.1 48.9 %all-to-all-start.2 = ((f32[32,104,128]{2,1,0:T(8,128)}), f32[32,104,128]{2,1,0:T(8,128)S(1)}, u32[]{:S(2)}, u32[]{:S(2)}) async-start(f32[32,104,128]{2,1,0:T(8,128)} %bitcast.10), calls=%async_computation.2 | async-start | bytes 3407872 | tf_op jit(solution)/shard_map/all_to_all | solution.py:249
  19.4 43.7 %copy-start.1 = (f32[8192]{0:T(1024)S(1)}, f32[8192]{0:T(1024)}, u32[]{:S(2)}) copy-start(f32[8192]{0:T(1024)} %param.11) | copy-start | bytes 98308
  63.1 2.2 %copy-start = (f32[8192,128]{1,0:T(8,128)S(1)}, f32[8192,128]{1,0:T(8,128)}, u32[]{:S(2)}) copy-start(f32[8192,128]{1,0:T(8,128)} %table_hbm.1) | copy-start | bytes 12582916

commit v2 on v1

--- a/solution.py
+++ b/solution.py
@@ -24,14 +24,20 @@
 
 
 def bin_kernel(
-    devices, rows_dev, ids_ref, map_ref, grad_hbm, send_ref, info_ref, grad_ref, cols, marks, target_vmem, target, sums, sems
+    devices, rows_dev, ids_hbm, map_hbm, grad_hbm, send_ref, info_ref, ids_ref, map_ref, grad_ref, cols, marks, target_vmem, target, sums, sems
 ):
     blocks = ids_ref.shape[0]
     width = send_ref.shape[0] // devices
     slots = width - 1
     drop = devices * width
     fetch = pltpu.make_async_copy(grad_hbm, grad_ref, sems.at[0])
+    fetch_ids = pltpu.make_async_copy(ids_hbm, ids_ref, sems.at[1])
+    fetch_map = pltpu.make_async_copy(map_hbm, map_ref, sems.at[2])
+    fetch_ids.start()
+    fetch_map.start()
     fetch.start()
+    fetch_ids.wait()
+    fetch_map.wait()
 
     block, within = split(ids_ref[...], BLOCK)
     high, low = split(block, LANES)
@@ -100,7 +106,7 @@
             ranks[b] = jnp.where(col == rows[b], mark, ranks[b])
     rank = jnp.concatenate([jnp.min(r, axis=0, keepdims=True) for r in ranks], axis=0)
     target_vmem[...] = jnp.where(rank < slots, owner * width + rank, drop)
-    send_target = pltpu.make_async_copy(target_vmem, target, sems.at[1])
+    send_target = pltpu.make_async_copy(target_vmem, target, sems.at[3])
     send_target.start()
     info_ref[0:blocks, :] = rank
     info_ref[blocks : 2 * blocks, :] = position
@@ -118,17 +124,12 @@
 
     @pl.loop(0, blocks)
     def _(b):
-        @pl.loop(0, LANES // UNROLL)
-        def _(q):
-            c0 = q * UNROLL
-            at = [target[b, c0 + u] for u in range(UNROLL)]
-            for g in range(0, UNROLL, STREAMS):
-                old = [sums[s][pl.ds(at[g + s], 1), :] for s in range(STREAMS)]
-                new = [
-                    old[s] + grad_ref[pl.ds(b * LANES + c0 + g + s, 1), :] for s in range(STREAMS)
-                ]
-                for s in range(STREAMS):
-                    sums[s][pl.ds(at[g + s], 1), :] = new[s]
+        for c0 in range(0, LANES, STREAMS):
+            at = [target[b, c0 + s] for s in range(STREAMS)]
+            old = [sums[s][pl.ds(at[s], 1), :] for s in range(STREAMS)]
+            new = [old[s] + grad_ref[pl.ds(b * LANES + c0 + s, 1), :] for s in range(STREAMS)]
+            for s in range(STREAMS):
+                sums[s][pl.ds(at[s], 1), :] = new[s]
 
     total = sums[0][0:drop, :]
     for s in range(1, STREAMS):
@@ -138,17 +139,19 @@
 
 
 def update_kernel(
-    devices, got_ref, more_head_ref, more_hbm, accum_ref, table_hbm, table_out, accum_out,
-    sums, table, more, head_vmem, head, sems_in, sems_out, sem,
+    devices, rounds, *refs
 ):
+    if rounds == 2:
+        more_head_ref, more_ref, *refs = refs
+    got_ref, accum_ref, table_hbm, table_out, accum_out, sums, table, head_vmem, head, sems_in, sems_out, sem = refs
     width = got_ref.shape[0] // devices
     slots = width - 1
-    more_width = more_hbm.shape[0] // devices
     rows_dev = table.shape[0]
     chunk = rows_dev // CHUNKS
     unroll = UNROLL if width % UNROLL == 0 else 8
     head_vmem[0:devices, :] = got_ref[pl.ds(slots, devices, stride=width), :].astype(jnp.int32)
-    head_vmem[devices : 2 * devices, :] = more_head_ref[...]
+    if rounds == 2:
+        head_vmem[devices : 2 * devices, :] = more_head_ref[...]
     load_head = pltpu.make_async_copy(head_vmem, head, sem)
     load_head.start()
     loads = [
@@ -162,46 +165,43 @@
     sums[...] = jnp.zeros_like(sums)
     load_head.wait()
 
-    def add_rows(source_head, rows_ref, base, count):
-        @pl.loop(0, lax.div(count + unroll - 1, unroll))
-        def _(q):
-            r0 = q * unroll
-            at = [head[source_head, r0 + u] for u in range(unroll)]
-            old = [sums[pl.ds(a, 1), :] for a in at]
-            new = [old[u] + rows_ref[pl.ds(base + r0 + u, 1), :] for u in range(unroll)]
-            for u in range(unroll):
-                sums[pl.ds(at[u], 1), :] = new[u]
+    def add_rows(source_head, rows_ref, base, limit):
+        count = head[source_head, LANES - 1]
+        for r0 in range(0, limit, unroll):
+
+            @pl.when(count > r0)
+            def _():
+                at = [head[source_head, r0 + u] for u in range(unroll)]
+                old = [sums[pl.ds(a, 1), :] for a in at]
+                new = [old[u] + rows_ref[pl.ds(base + r0 + u, 1), :] for u in range(unroll)]
+                for u in range(unroll):
+                    sums[pl.ds(at[u], 1), :] = new[u]
 
     @pl.loop(0, devices)
     def _(d):
-        add_rows(d, got_ref, d * width, head[d, LANES - 1])
-
-    @pl.loop(0, devices)
-    def _(d):
-        @pl.when(head[devices + d, LANES - 1] > 0)
-        def _():
-            copy = pltpu.make_async_copy(
-                more_hbm.at[pl.ds(d * more_width, more_width), :], more.at[pl.ds(0, more_width), :], sem
-            )
-            copy.start()
-            copy.wait()
-            add_rows(devices + d, more, 0, head[devices + d, LANES - 1])
+        add_rows(d, got_ref, d * width, slots)
+
+    if rounds == 2:
+        more_width = more_ref.shape[0] // devices
+
+        @pl.loop(0, devices)
+        def _(d):
+            add_rows(devices + d, more_ref, d * more_width, more_width)
 
     groups = chunk // LANES
     stores = []
     for c in range(CHUNKS):
+        heres = [pl.ds((c * groups + i) * LANES, LANES) for i in range(groups)]
+        these = pl.ds(c * groups, groups)
+        squares = [jnp.transpose(jnp.square(sums[here, :])) for here in heres]
+        totals = jnp.concatenate([jnp.sum(x, axis=0, keepdims=True) for x in squares], axis=0)
+        new_accum = accum_ref[these, :] + totals * (1.0 / LANES)
+        accum_out[these, :] = new_accum
+        scale = learning_rate / (jnp.sqrt(new_accum) + epsilon)
         loads[c].wait()
-
-        @pl.loop(0, groups)
-        def _(i):
-            k = c * groups + i
-            here = pl.ds(pl.multiple_of(k * LANES, LANES), LANES)
-            grad = sums[here, :]
-            mean = jnp.sum(jnp.transpose(grad * grad), axis=0, keepdims=True) * (1.0 / LANES)
-            new_accum = accum_ref[pl.ds(k, 1), :] + mean
-            accum_out[pl.ds(k, 1), :] = new_accum
-            scale = learning_rate / (jnp.sqrt(new_accum) + epsilon)
-            table[here, :] = table[here, :] - jnp.transpose(jnp.broadcast_to(scale, (LANES, LANES))) * grad
+        for i, here in enumerate(heres):
+            factor = jnp.transpose(jnp.broadcast_to(scale[i : i + 1, :], (LANES, LANES)))
+            table[here, :] = table[here, :] - factor * sums[here, :]
 
         store = pltpu.make_async_copy(
             table.at[pl.ds(c * chunk, chunk), :], table_out.at[pl.ds(c * chunk, chunk), :], sems_out.at[c]
@@ -223,7 +223,7 @@
     more_slots = -(-(capacity - slots) // UNROLL) * UNROLL
     blocks = look_count // LANES
     vmem = pl.BlockSpec(memory_space=pltpu.VMEM)
-    hbm = pl.BlockSpec(memory_space=pl.ANY)
+    hbm = pl.BlockSpec(memory_space=pltpu.MemorySpace.HBM)
 
     send, info = pl.pallas_call(
         functools.partial(bin_kernel, devices, rows_dev),
@@ -231,16 +231,18 @@
             jax.ShapeDtypeStruct((devices * width, features), jnp.float32),
             jax.ShapeDtypeStruct((2 * blocks, LANES), jnp.int32),
         ),
-        in_specs=[vmem, vmem, hbm],
+        in_specs=[hbm, hbm, hbm],
         out_specs=(vmem, vmem),
         scratch_shapes=[
+            pltpu.VMEM((blocks, LANES), jnp.int32),
+            pltpu.VMEM((block_map.shape[0] // LANES, LANES), jnp.int32),
             pltpu.VMEM((look_count, features), jnp.float32),
             pltpu.VMEM((look_count, LANES), jnp.int32),
             pltpu.VMEM((look_count, LANES), jnp.int32),
             pltpu.VMEM((blocks, LANES), jnp.int32),
             pltpu.SMEM((blocks, LANES), jnp.int32),
             [pltpu.VMEM((devices * width + 8, features), jnp.float32)] * STREAMS,
-            pltpu.SemaphoreType.DMA((2,)),
+            pltpu.SemaphoreType.DMA((4,)),
         ],
         compiler_params=pltpu.CompilerParams(vmem_limit_bytes=24 << 20),
         name="bin_rows",
@@ -248,7 +250,30 @@
 
     got = lax.all_to_all(send, axes, split_axis=0, concat_axis=0, tiled=True)
 
-    def second_round(_):
+    def apply_step(rounds, *args):
+        new_table, new_accum = pl.pallas_call(
+            functools.partial(update_kernel, devices, rounds),
+            out_shape=(
+                jax.ShapeDtypeStruct(table.shape, jnp.float32),
+                jax.ShapeDtypeStruct((rows_dev // LANES, LANES), jnp.float32),
+            ),
+            in_specs=[vmem] * (2 * rounds) + [hbm],
+            out_specs=(hbm, vmem),
+            scratch_shapes=[
+                pltpu.VMEM((rows_dev + 8, features), jnp.float32),
+                pltpu.VMEM((rows_dev, features), jnp.float32),
+                pltpu.VMEM((rounds * devices, LANES), jnp.int32),
+                pltpu.SMEM((rounds * devices, LANES), jnp.int32),
+                pltpu.SemaphoreType.DMA((CHUNKS,)),
+                pltpu.SemaphoreType.DMA((CHUNKS,)),
+                pltpu.SemaphoreType.DMA(()),
+            ],
+            compiler_params=pltpu.CompilerParams(vmem_limit_bytes=24 << 20),
+            name=f"apply_step_{rounds}",
+        )(*args, got, accum.reshape(-1, LANES), table)
+        return new_table, new_accum.reshape(-1)
+
+    def two_rounds():
         rank, position = info[:blocks].reshape(-1), info[blocks:].reshape(-1)
         owner, slot = position // rows_dev, position % rows_dev
         limit = devices * more_slots
@@ -260,39 +285,10 @@
         places = places.reshape(devices, more_slots)
         count = jnp.sum((places < rows_dev).astype(jnp.int32), axis=1, keepdims=True)
         places = jnp.pad(places, ((0, 0), (0, LANES - 1 - more_slots)), constant_values=rows_dev)
-        return rows, jnp.concatenate([places, count], axis=1)
-
-    def one_round(_):
-        return (
-            jnp.zeros((devices * more_slots, features), jnp.float32),
-            jnp.zeros((devices, LANES), jnp.int32),
-        )
+        return apply_step(2, jnp.concatenate([places, count], axis=1), rows)
 
     over = jnp.max(got.reshape(devices, width, features)[:, slots, LANES - 2]) > 0.5
-    more, more_head = lax.cond(over, second_round, one_round, None)
-
-    new_table, new_accum = pl.pallas_call(
-        functools.partial(update_kernel, devices),
-        out_shape=(
-            jax.ShapeDtypeStruct(table.shape, jnp.float32),
-            jax.ShapeDtypeStruct((rows_dev // LANES, LANES), jnp.float32),
-        ),
-        in_specs=[vmem, vmem, hbm, vmem, hbm],
-        out_specs=(hbm, vmem),
-        scratch_shapes=[
-            pltpu.VMEM((rows_dev + 8, features), jnp.float32),
-            pltpu.VMEM((rows_dev, features), jnp.float32),
-            pltpu.VMEM((more_slots + UNROLL, features), jnp.float32),
-            pltpu.VMEM((2 * devices, LANES), jnp.int32),
-            pltpu.SMEM((2 * devices, LANES), jnp.int32),
-            pltpu.SemaphoreType.DMA((CHUNKS,)),
-            pltpu.SemaphoreType.DMA((CHUNKS,)),
-            pltpu.SemaphoreType.DMA(()),
-        ],
-        compiler_params=pltpu.CompilerParams(vmem_limit_bytes=24 << 20),
-        name="apply_step",
-    )(got, more_head, more, accum.reshape(-1, LANES), table)
-    return new_table, new_accum.reshape(-1)
+    return lax.cond(over, two_rounds, lambda: apply_step(1))
 
 
 def solution(mesh):

time: 88.6 us -> 68 us (0.77)
  blocking collectives: 0 us -> 48.6 us
  waiting for transfers between devices: 41.5 us -> 0 us
  Pallas kernels: 32.8 us -> 15.7 us
  starting transfers between devices: 7.33 us -> 0 us
  local copies, waits for them, and re-layouts: 4.42 us -> 1.39 us
    all_to_all x0 -> x1, blocking collectives: none -> 48.6 us  [on_device(): got = lax.all_to_all(send, axes, split_axis=0, concat_axis=0, tiled=True)]
    all_to_all x1 -> x0, waiting for transfers between devices: 41.5 us -> none  [on_device(): got = lax.all_to_all(send, axes, split_axis=0, concat_axis=0, tiled=True)]
    pallas_call x1, Pallas kernels: 22.8 us -> 9.78 us  [apply_step(): pl.pallas_call(functools.partial(update_kernel, devices, rounds), out_sha...]
    all_to_all x1 -> x0, starting transfers between devices: 7.33 us -> none  [on_device(): got = lax.all_to_all(send, axes, split_axis=0, concat_axis=0, tiled=True)]
    pallas_call x1, Pallas kernels: 10 us -> 5.88 us  [on_device(): pl.pallas_call(functools.partial(bin_kernel, devices, rows_dev), out_shap...]
    unnamed x8 -> x6, local copies, waits for them, and re-layouts: 3.58 us -> 1.39 us
  transfers between devices with their start and end apart: 1 -> 0, of which waited for: 1 -> 0; matrix products, arithmetic and copies ran while one was open for 0% -> 0% of each run, Pallas kernels for 0% -> 0%
where the time goes in v2:
time: 68 us; the launch traced here: 67.7 us
  blocking collectives  48.6 us (71%)
  Pallas kernels  15.7 us (23%)
  local copies, waits for them, and re-layouts  1.39 us (2%)
  between operations  1.31 us (2%)
  other arithmetic  0.7 us (1%)
    all_to_all x1, blocking collectives, on_device(): got = lax.all_to_all(send, axes, split_axis=0, concat_axis=0, tiled=True)  48.6 us
    pallas_call x1, Pallas kernels, apply_step(): pl.pallas_call(functools.partial(update_kernel, devices, rounds), out_sha...  9.78 us
    pallas_call x1, Pallas kernels, on_device(): pl.pallas_call(functools.partial(bin_kernel, devices, rows_dev), out_shap...  5.88 us
    unnamed x6, local copies, waits for them, and re-layouts  1.39 us

profile of v2, /device:TPU:0, one launch (start us, length us, event | category | flops | bytes accessed | tf_op | source)
XLA Modules:
  0.0 67.7 jit_solution(18328928536705467935)
XLA Ops:
  0.6 0.0 copy-start
  0.6 0.7 %copy-done = s32[2048]{0:T(1024)S(1)} copy-done((s32[2048]{0:T(1024)S(1)}, s32[2048]{0:T(1024)}, u32[]{:S(2)}) %copy-start) | copy-done | bytes 8216
  1.3 0.0 copy-start.1
  1.3 0.7 %copy-done.1 = s32[2048]{0:T(1024)S(1)} copy-done((s32[2048]{0:T(1024)S(1)}, s32[2048]{0:T(1024)}, u32[]{:S(2)}) %copy-start.1) | copy-done | bytes 8216
  2.0 0.0 copy-start.2
  2.0 5.9 %bin_rows.1 = (f32[3328,128]{1,0:T(8,128)S(1)}, s32[32,128]{1,0:T(8,128)S(1)}) custom-call(s32[16,128]{1,0:T(8,128)S(1)} %bitcast.22, s32[16,128]{1,0:T(8,128)S(1)} %bitcast.23, f32[2048,128]{1,0:T(8,128)} %grad_hbm.1), custom_call_target="tpu_custom_call" | custom-call | tf_op jit(solution)/shard_map/bin_rows/pallas_call | solution.py:228
  7.9 48.6 %all_to_all.27 = f32[32,104,128]{2,1,0:T(8,128)S(1)} all-to-all(f32[32,104,128]{2,1,0:T(8,128)S(1)} %bitcast.21), channel_id=1, replica_groups=mesh['gx'=4,'gy'=8] {'gx','gy'}, dimensions={0} | all-to-all | bytes 3407872 | tf_op jit(solution)/shard_map/all_to_all | solution.py:251
  56.6 0.7 %slice_reduce_fusion = f32[]{:T(128)} fusion(f32[32,104,128]{2,1,0:T(8,128)S(1)} %all_to_all.27), kind=kLoop, calls=%fused_computation.19 | loop fusion | flops 31 | bytes 132 | tf_op jit(solution)/shard_map/reduce_max | solution.py:290
  57.9 0.0 copy-done.2
  57.9 9.8 %conditional.1 = (f32[8192,128]{1,0:T(8,128)}, f32[8192]{0:T(1024)}) conditional(s32[]{:T(128)} %convert_element_type.6, (f32[8192]{0:T(1024)S(1)}, f32[3328,128]{1,0:T(8,128)S(1)}, f32[8192,128]{1,0:T(8,128)}) %tuple.24, (s32[32,128]{1,0:T(8,128)S(1)}, f32[2048,128]{1,0:T(8,128)}, f32[8192]{0:T(1024)S(1)}, f32[3328,128]{1,0:T(8,128)S(1)}, ...), branch_computations={%region_1.0_spmd, %region_2.6_spmd} | conditional | flops 347104 | bytes 2245716 | solution.py:291
  57.9 9.8 %apply_step_1.1 = (f32[8192,128]{1,0:T(8,128)}, f32[64,128]{1,0:T(8,128)}) custom-call(f32[3328,128]{1,0:T(8,128)S(1)} %get-tuple-element.16.refs_0_, f32[64,128]{1,0:T(8,128)S(1)} %bitcast.28, f32[8192,128]{1,0:T(8,128)} %get-tuple-element.18.refs_2_), custom_call_target="tpu_custom_call" | custom-call | tf_op jit(solution)/shard_map/cond/branch_0_fun/apply_step_1/pallas_call | solution.py:254
Async XLA Ops:
  0.6 0.7 %copy-start = (s32[2048]{0:T(1024)S(1)}, s32[2048]{0:T(1024)}, u32[]{:S(2)}) copy-start(s32[2048]{0:T(1024)} %param.7) | copy-start | bytes 24580
  1.3 0.7 %copy-start.1 = (s32[2048]{0:T(1024)S(1)}, s32[2048]{0:T(1024)}, u32[]{:S(2)}) copy-start(s32[2048]{0:T(1024)} %param.8) | copy-start | bytes 24580
  2.0 55.9 %copy-start.2 = (f32[8192]{0:T(1024)S(1)}, f32[8192]{0:T(1024)}, u32[]{:S(2)}) copy-start(f32[8192]{0:T(1024)} %param.11) | copy-start | bytes 98308

commit v3 on v2

--- a/solution.py
+++ b/solution.py
@@ -24,7 +24,7 @@
 
 
 def bin_kernel(
-    devices, rows_dev, ids_hbm, map_hbm, grad_hbm, send_ref, info_ref, ids_ref, map_ref, grad_ref, cols, marks, target_vmem, target, sums, sems
+    devices, group, spare, rows_dev, ids_hbm, map_hbm, grad_hbm, send_ref, info_ref, ids_ref, map_ref, grad_ref, cols, marks, target_vmem, target, sums, sems
 ):
     blocks = ids_ref.shape[0]
     width = send_ref.shape[0] // devices
@@ -76,21 +76,44 @@
     ahead = ((i0 < i1)).astype(jnp.float32).astype(jnp.bfloat16)
     counted = jnp.dot(hot16, ahead, preferred_element_type=jnp.float32)
     counts = jnp.zeros((devices, LANES), jnp.float32)
+    ranks = []
+    for b in range(blocks):
+        here = counted[b * devices : (b + 1) * devices]
+        ranks.append(jnp.sum(jnp.where(owned[b], here[:, :LANES] + counts, 0.0), axis=0, keepdims=True))
+        counts = counts + here[:, LANES:]
+
+    def partner(x):
+        parts = [x[i : i + group] for i in range(0, devices, group)]
+        return jnp.concatenate([parts[i ^ 1] for i in range(len(parts))], axis=0)
+
+    kept = jnp.minimum(counts, slots)
+    extra = counts - kept
+    fits = (extra <= spare) & (partner(kept) + extra <= slots)
+    shift = jnp.where(fits, slots - counts, -2.0 * LANES)
+    guests = partner(jnp.where(fits, extra, 0.0))
+
     header_high = jnp.zeros((devices, LANES), jnp.float32)
     header_low = jnp.zeros((devices, LANES), jnp.float32)
     slot_high, slot_low = split(slot, LANES)
     lanes = lax.broadcasted_iota(jnp.int32, (LANES, LANES), 1)
+    nowhere = devices * LANES
     for b in range(blocks):
-        here = counted[b * devices : (b + 1) * devices]
-        rank = jnp.sum(jnp.where(owned[b], here[:, :LANES] + counts, 0.0), axis=0, keepdims=True)
-        counts = counts + here[:, LANES:]
-        rank_col = column(rank.astype(jnp.int32))
-        marks[b * LANES : (b + 1) * LANES, :] = rank_col
-        place = (rank_col == lanes).astype(jnp.float32).astype(jnp.bfloat16)
+        moved = ranks[b] + jnp.sum(jnp.where(owned[b], shift, 0.0), axis=0, keepdims=True)
+        at_home = ranks[b] < slots
+        mine = owner[b : b + 1, :]
+        across, _ = split(mine, group)
+        other = mine + jnp.where((across & 1) == 0, group, -group)
+        bin_of = jnp.where(at_home, mine, jnp.where(moved >= 0.0, other, devices))
+        row_of = jnp.where(at_home, ranks[b], jnp.where(moved >= 0.0, moved, 0.0)).astype(jnp.int32)
+        bin_of = jnp.where(leads[b], bin_of, devices)
+        mark_col = column(jnp.where(bin_of < devices, bin_of * LANES + row_of, nowhere))
+        marks[b * LANES : (b + 1) * LANES, :] = mark_col
+        place = ((mark_col & (LANES - 1)) == lanes).astype(jnp.float32).astype(jnp.bfloat16)
+        sent = device == bin_of
         both = jnp.concatenate(
             [
-                jnp.where(hot[b], slot_high[b : b + 1, :].astype(jnp.float32), 0.0),
-                jnp.where(hot[b], slot_low[b : b + 1, :].astype(jnp.float32), 0.0),
+                jnp.where(sent, slot_high[b : b + 1, :].astype(jnp.float32), 0.0),
+                jnp.where(sent, slot_low[b : b + 1, :].astype(jnp.float32), 0.0),
             ],
             axis=0,
         ).astype(jnp.bfloat16)
@@ -98,27 +121,28 @@
         header_high = header_high + parts[:devices]
         header_low = header_low + parts[devices:]
 
-    ranks = [jnp.full((8, LANES), drop, jnp.int32) for _ in range(blocks)]
+    best = [jnp.full((8, LANES), nowhere, jnp.int32) for _ in range(blocks)]
     for v in reversed(range(blocks * per_block)):
         col = cols[8 * v : 8 * v + 8, :]
         mark = marks[8 * v : 8 * v + 8, :]
         for b in range(v // per_block, blocks):
-            ranks[b] = jnp.where(col == rows[b], mark, ranks[b])
-    rank = jnp.concatenate([jnp.min(r, axis=0, keepdims=True) for r in ranks], axis=0)
-    target_vmem[...] = jnp.where(rank < slots, owner * width + rank, drop)
+            best[b] = jnp.where(col == rows[b], jnp.minimum(mark, best[b]), best[b])
+    mark = jnp.concatenate([jnp.min(x, axis=0, keepdims=True) for x in best], axis=0)
+    target_vmem[...] = jnp.where(
+        mark < nowhere, lax.shift_right_logical(mark, 7) * width + (mark & (LANES - 1)), drop
+    )
     send_target = pltpu.make_async_copy(target_vmem, target, sems.at[3])
     send_target.start()
-    info_ref[0:blocks, :] = rank
+    info_ref[0:blocks, :] = mark
     info_ref[blocks : 2 * blocks, :] = position
 
     for s in range(STREAMS):
         sums[s][...] = jnp.zeros_like(sums[s])
-    over = jnp.max(counts) > slots
-    header = jnp.where(
-        lane.astype(jnp.float32) < jnp.minimum(counts, slots), header_high * LANES + header_low, float(rows_dev)
-    )
-    header = jnp.where(lane == LANES - 1, jnp.minimum(counts, slots), header)
-    header = jnp.where(lane == LANES - 2, jnp.where(over, 1.0, 0.0), header)
+    over = jnp.max(jnp.where(fits, 0.0, 1.0))
+    header = header_high * LANES + header_low
+    header = jnp.where(lane == LANES - 1, kept, header)
+    header = jnp.where(lane == LANES - 2, over, header)
+    header = jnp.where(lane == LANES - 3, guests, header)
     send_target.wait()
     fetch.wait()
 
@@ -143,15 +167,24 @@
 ):
     if rounds == 2:
         more_head_ref, more_ref, *refs = refs
-    got_ref, accum_ref, table_hbm, table_out, accum_out, sums, table, head_vmem, head, sems_in, sems_out, sem = refs
+    got_ref, guest_ref, accum_ref, table_hbm, table_out, accum_out, sums, table, head_vmem, head, sems_in, sems_out, sem = refs
     width = got_ref.shape[0] // devices
     slots = width - 1
     rows_dev = table.shape[0]
     chunk = rows_dev // CHUNKS
     unroll = UNROLL if width % UNROLL == 0 else 8
-    head_vmem[0:devices, :] = got_ref[pl.ds(slots, devices, stride=width), :].astype(jnp.int32)
+    guest_width = guest_ref.shape[0] // devices
+    lane = lax.broadcasted_iota(jnp.int32, (devices, LANES), 1)
+    last = LANES - 1
+    own = got_ref[pl.ds(slots, devices, stride=width), :].astype(jnp.int32)
+    head_vmem[0:devices, :] = jnp.where((lane < own[:, last:]) | (lane == last), own, rows_dev)
+    guest = guest_ref[pl.ds(guest_width - 1, devices, stride=guest_width), :].astype(jnp.int32)
+    guests = guest[:, last - 2 : last - 1]
+    head_vmem[devices : 2 * devices, :] = jnp.where(
+        lane == last, guests, jnp.where((lane >= slots - guests) & (lane < slots), guest, rows_dev)
+    )
     if rounds == 2:
-        head_vmem[devices : 2 * devices, :] = more_head_ref[...]
+        head_vmem[2 * devices : 3 * devices, :] = more_head_ref[...]
     load_head = pltpu.make_async_copy(head_vmem, head, sem)
     load_head.start()
     loads = [
@@ -165,28 +198,38 @@
     sums[...] = jnp.zeros_like(sums)
     load_head.wait()
 
-    def add_rows(source_head, rows_ref, base, limit):
-        count = head[source_head, LANES - 1]
+    def add_group(source, c0, rows_ref, base, size):
+        at = [head[source, c0 + u] for u in range(size)]
+        old = [sums[pl.ds(a, 1), :] for a in at]
+        new = [old[u] + rows_ref[pl.ds(base + u, 1), :] for u in range(size)]
+        for u in range(size):
+            sums[pl.ds(at[u], 1), :] = new[u]
+
+    def add_rows(source, rows_ref, base, limit):
+        count = head[source, LANES - 1]
         for r0 in range(0, limit, unroll):
 
             @pl.when(count > r0)
             def _():
-                at = [head[source_head, r0 + u] for u in range(unroll)]
-                old = [sums[pl.ds(a, 1), :] for a in at]
-                new = [old[u] + rows_ref[pl.ds(base + r0 + u, 1), :] for u in range(unroll)]
-                for u in range(unroll):
-                    sums[pl.ds(at[u], 1), :] = new[u]
+                add_group(source, r0, rows_ref, base + r0, unroll)
 
     @pl.loop(0, devices)
     def _(d):
         add_rows(d, got_ref, d * width, slots)
+        guests = head[devices + d, LANES - 1]
+        for r0 in range(guest_width - 8, -1, -8):
+
+            @pl.when(guests > max(guest_width - 9 - r0, 0))
+            def _():
+                add_group(devices + d, width - guest_width + r0, guest_ref, d * guest_width + r0, 8)
+
 
     if rounds == 2:
         more_width = more_ref.shape[0] // devices
 
         @pl.loop(0, devices)
         def _(d):
-            add_rows(devices + d, more_ref, d * more_width, more_width)
+            add_rows(2 * devices + d, more_ref, d * more_width, more_width)
 
     groups = chunk // LANES
     stores = []
@@ -218,7 +261,8 @@
     rows_dev, features = table.shape
     look_count = row_ids.shape[0]
     capacity = 2 * look_count // devices
-    width = -(-capacity * 13 // 16 // 8) * 8
+    width = -(-capacity * 5 // 8 // 8) * 8
+    guest_width = -(-width * 3 // 10 // 8) * 8
     slots = width - 1
     more_slots = -(-(capacity - slots) // UNROLL) * UNROLL
     blocks = look_count // LANES
@@ -226,7 +270,7 @@
     hbm = pl.BlockSpec(memory_space=pltpu.MemorySpace.HBM)
 
     send, info = pl.pallas_call(
-        functools.partial(bin_kernel, devices, rows_dev),
+        functools.partial(bin_kernel, devices, lax.axis_size("gy"), guest_width - 1, rows_dev),
         out_shape=(
             jax.ShapeDtypeStruct((devices * width, features), jnp.float32),
             jax.ShapeDtypeStruct((2 * blocks, LANES), jnp.int32),
@@ -249,6 +293,9 @@
     )(row_ids.reshape(blocks, LANES), block_map.reshape(-1, LANES), grad_tiles)
 
     got = lax.all_to_all(send, axes, split_axis=0, concat_axis=0, tiled=True)
+    guests = got.reshape(devices, width, features)[:, width - guest_width :, :]
+    guests = lax.ppermute(guests, "gx", [(i, i ^ 1) for i in range(lax.axis_size("gx"))])
+    guests = guests.reshape(devices * guest_width, features)
 
     def apply_step(rounds, *args):
         new_table, new_accum = pl.pallas_call(
@@ -257,27 +304,34 @@
                 jax.ShapeDtypeStruct(table.shape, jnp.float32),
                 jax.ShapeDtypeStruct((rows_dev // LANES, LANES), jnp.float32),
             ),
-            in_specs=[vmem] * (2 * rounds) + [hbm],
+            in_specs=[vmem] * (2 * rounds + 1) + [hbm],
             out_specs=(hbm, vmem),
             scratch_shapes=[
                 pltpu.VMEM((rows_dev + 8, features), jnp.float32),
                 pltpu.VMEM((rows_dev, features), jnp.float32),
-                pltpu.VMEM((rounds * devices, LANES), jnp.int32),
-                pltpu.SMEM((rounds * devices, LANES), jnp.int32),
+                pltpu.VMEM(((rounds + 1) * devices, LANES), jnp.int32),
+                pltpu.SMEM(((rounds + 1) * devices, LANES), jnp.int32),
                 pltpu.SemaphoreType.DMA((CHUNKS,)),
                 pltpu.SemaphoreType.DMA((CHUNKS,)),
                 pltpu.SemaphoreType.DMA(()),
             ],
             compiler_params=pltpu.CompilerParams(vmem_limit_bytes=24 << 20),
             name=f"apply_step_{rounds}",
-        )(*args, got, accum.reshape(-1, LANES), table)
+        )(*args, got, guests, accum.reshape(-1, LANES), table)
         return new_table, new_accum.reshape(-1)
 
     def two_rounds():
-        rank, position = info[:blocks].reshape(-1), info[blocks:].reshape(-1)
+        mark, position = info[:blocks].reshape(-1), info[blocks:].reshape(-1)
         owner, slot = position // rows_dev, position % rows_dev
         limit = devices * more_slots
-        at = jnp.where(rank >= slots, owner * more_slots + rank - slots, limit)
+        left = mark >= devices * LANES
+        lookup = jnp.arange(look_count, dtype=jnp.int32)
+        same = left[:, None] & left[None, :] & (position[:, None] == position[None, :])
+        first = jnp.min(jnp.where(same, lookup[None, :], look_count), axis=1)
+        lead = left & (first == lookup)
+        before = lead[None, :] & (owner[:, None] == owner[None, :]) & (lookup[None, :] < first[:, None])
+        rank = jnp.sum(before.astype(jnp.int32), axis=1)
+        at = jnp.where(left, owner * more_slots + rank, limit)
         rows = jnp.zeros((limit, features), jnp.float32).at[at].add(grad_tiles, mode="drop")
         places = jnp.full((limit,), rows_dev, jnp.int32).at[at].set(slot, mode="drop")
         rows = lax.all_to_all(rows, axes, split_axis=0, concat_axis=0, tiled=True)

time: 68 us -> 61.2 us (0.900)
  blocking collectives: 48.6 us -> 40.2 us
  Pallas kernels: 15.7 us -> 16.4 us
    all_to_all x1, blocking collectives: 48.6 us -> 40.2 us  [on_device(): got = lax.all_to_all(send, axes, split_axis=0, concat_axis=0, tiled=True)]
  transfers between devices with their start and end apart: 0 -> 1, of which waited for: 0 -> 1; matrix products, arithmetic and copies ran while one was open for 0% -> 1% of each run, Pallas kernels for 0% -> 0%
where the time goes in v3:
time: 61.2 us; the launch traced here: 60.9 us
  blocking collectives  40.2 us (66%)
  Pallas kernels  16.4 us (27%)
  between operations  1.5 us (2%)
  local copies, waits for them, and re-layouts  1.42 us (2%)
  other arithmetic  0.7 us (1%)
    all_to_all x1, blocking collectives, on_device(): got = lax.all_to_all(send, axes, split_axis=0, concat_axis=0, tiled=True)  40.2 us
    pallas_call x1, Pallas kernels, apply_step(): pl.pallas_call(functools.partial(update_kernel, devices, rounds), out_sha...  9.94 us
    pallas_call x1, Pallas kernels, on_device(): pl.pallas_call(functools.partial(bin_kernel, devices, lax.axis_size('gy')...  6.47 us
    unnamed x6, local copies, waits for them, and re-layouts  1.39 us
  transfers between devices with their start and end apart: 1, of which 1 were waited for; matrix products, arithmetic and copies ran while one was open for 1% of the time, Pallas kernels for 0%

profile of v3, /device:TPU:0, one launch (start us, length us, event | category | flops | bytes accessed | tf_op | source)
XLA Modules:
  0.0 60.9 jit_solution(14582688178546687177)
XLA Ops:
  0.6 0.0 copy-start
  0.6 0.7 %copy-done = s32[2048]{0:T(1024)S(1)} copy-done((s32[2048]{0:T(1024)S(1)}, s32[2048]{0:T(1024)}, u32[]{:S(2)}) %copy-start) | copy-done | bytes 8216
  1.3 0.0 copy-start.1
  1.3 0.7 %copy-done.1 = s32[2048]{0:T(1024)S(1)} copy-done((s32[2048]{0:T(1024)S(1)}, s32[2048]{0:T(1024)}, u32[]{:S(2)}) %copy-start.1) | copy-done | bytes 8216
  2.0 0.0 copy-start.2
  2.0 6.5 %bin_rows.1 = (f32[2560,128]{1,0:T(8,128)S(1)}, s32[32,128]{1,0:T(8,128)S(1)}) custom-call(s32[16,128]{1,0:T(8,128)S(1)} %bitcast.34, s32[16,128]{1,0:T(8,128)S(1)} %bitcast.35, f32[2048,128]{1,0:T(8,128)} %grad_hbm.1), custom_call_target="tpu_custom_call" | custom-call | tf_op jit(solution)/shard_map/bin_rows/pallas_call | solution.py:272
  8.5 40.2 %all_to_all.27 = f32[32,80,128]{2,1,0:T(8,128)S(1)} all-to-all(f32[32,80,128]{2,1,0:T(8,128)S(1)} %bitcast.33), channel_id=1, replica_groups=mesh['gx'=4,'gy'=8] {'gx','gy'}, dimensions={0} | all-to-all | bytes 2621440 | tf_op jit(solution)/shard_map/all_to_all | solution.py:295
  48.8 0.1 collective-permute-start
  48.8 0.7 %slice_reduce_fusion = f32[]{:T(128)} fusion(f32[32,80,128]{2,1,0:T(8,128)S(1)} %all_to_all.27), kind=kLoop, calls=%fused_computation.31 | loop fusion | flops 31 | bytes 132 | tf_op jit(solution)/shard_map/reduce_max | solution.py:344
  50.2 0.4 collective-permute-done
  50.5 0.0 copy-done.2
  50.5 10.2 %conditional.1 = (f32[8192,128]{1,0:T(8,128)}, f32[8192]{0:T(1024)}) conditional(s32[]{:T(128)} %convert_element_type.9, (f32[8192]{0:T(1024)S(1)}, f32[2560,128]{1,0:T(8,128)S(1)}, f32[768,128]{1,0:T(8,128)S(1)}, f32[8192,128]{1,0:T(8,128)}) %tuple.27, (s32[32,128]{1,0:T(8,128)S(1)}, f32[2048,128]{1,0:T(8,128)}, f32[8192]{0:T(1024)S(1)}, ...), branch_computations={%region_1.0_spmd, %region_2.8_spmd} | conditional | flops 46505952 | bytes 4453460 | solution.py:345
  50.5 9.9 %apply_step_1.1 = (f32[8192,128]{1,0:T(8,128)}, f32[64,128]{1,0:T(8,128)}) custom-call(f32[2560,128]{1,0:T(8,128)S(1)} %get-tuple-element.20.refs_0_, f32[768,128]{1,0:T(8,128)S(1)} %get-tuple-element.21.refs_1_, f32[64,128]{1,0:T(8,128)S(1)} %bitcast.42, f32[8192,128]{1,0:T(8,128)} %get-tuple-element.23.refs_3_), custom_call_target="tpu_custom_call" | custom-call | tf_op jit(solution)/shard_map/cond/branch_0_fun/apply_step_1/pallas_call | solution.py:301
  (1 shorter events, 0.0 us)
Async XLA Ops:
  0.6 0.7 %copy-start = (s32[2048]{0:T(1024)S(1)}, s32[2048]{0:T(1024)}, u32[]{:S(2)}) copy-start(s32[2048]{0:T(1024)} %param.7) | copy-start | bytes 24580
  1.3 0.7 %copy-start.1 = (s32[2048]{0:T(1024)S(1)}, s32[2048]{0:T(1024)}, u32[]{:S(2)}) copy-start(s32[2048]{0:T(1024)} %param.8) | copy-start | bytes 24580
  2.0 48.5 %copy-start.2 = (f32[8192]{0:T(1024)S(1)}, f32[8192]{0:T(1024)}, u32[]{:S(2)}) copy-start(f32[8192]{0:T(1024)} %param.11) | copy-start | bytes 98308
  48.8 1.8 %collective-permute-start = (f32[32,24,128]{2,1,0:T(8,128)S(1)}, f32[32,24,128]{2,1,0:T(8,128)S(1)}, u32[]{:S(2)}, u32[]{:S(2)}) collective-permute-start(f32[32,24,128]{2,1,0:T(8,128)S(1)} %slice.15), channel_id=1, source_target_pairs={{0,8},{8,0},{16,24},{24,16},{1,9},{9,1},{17,25},{25,17},{2,10},{10... | collective-permute-start | bytes 1179656 | tf_op jit(solution)/shard_map/ppermute | solution.py:297

commit v4 on v3

--- a/solution.py
+++ b/solution.py
@@ -9,8 +9,9 @@
 
 BLOCK = 128
 LANES = 128
-STREAMS = 4
-UNROLL = 16
+STREAMS = 8
+GROUP = 8
+BATCH = 16
 CHUNKS = 8
 
 learning_rate = 0.25
@@ -172,7 +173,6 @@
     slots = width - 1
     rows_dev = table.shape[0]
     chunk = rows_dev // CHUNKS
-    unroll = UNROLL if width % UNROLL == 0 else 8
     guest_width = guest_ref.shape[0] // devices
     lane = lax.broadcasted_iota(jnp.int32, (devices, LANES), 1)
     last = LANES - 1
@@ -195,48 +195,58 @@
     ]
     for load in loads:
         load.start()
-    sums[...] = jnp.zeros_like(sums)
+    for k in range(2):
+        sums[k][...] = jnp.zeros_like(sums[k])
     load_head.wait()
 
-    def add_group(source, c0, rows_ref, base, size):
-        at = [head[source, c0 + u] for u in range(size)]
-        old = [sums[pl.ds(a, 1), :] for a in at]
-        new = [old[u] + rows_ref[pl.ds(base + u, 1), :] for u in range(size)]
-        for u in range(size):
-            sums[pl.ds(at[u], 1), :] = new[u]
-
-    def add_rows(source, rows_ref, base, limit):
-        count = head[source, LANES - 1]
-        for r0 in range(0, limit, unroll):
+    def add_pair(section, d, c0, rows_ref, first, step, size):
+        spots = [[head[section * devices + d + k, c0 + u] for u in range(size)] for k in range(2)]
+        plan = [(k, u) for u in range(0, size, GROUP) for k in range(2)]
+        late = []
+        for k, u0 in plan:
+            now = []
+            for u in range(u0, min(u0 + GROUP, size)):
+                here = pl.ds(spots[k][u], 1)
+                now.append((k, here, sums[k][here, :] + rows_ref[pl.ds(first + k * step + u, 1), :]))
+                if late:
+                    j, there, value = late.pop(0)
+                    sums[j][there, :] = value
+            for j, there, value in late:
+                sums[j][there, :] = value
+            late = now
+        for j, there, value in late:
+            sums[j][there, :] = value
+
+    def add_rows(section, d, rows_ref, width):
+        count = jnp.maximum(head[section * devices + d, last], head[section * devices + d + 1, last])
+        for r0 in range(0, width, BATCH):
 
             @pl.when(count > r0)
             def _():
-                add_group(source, r0, rows_ref, base + r0, unroll)
-
-    @pl.loop(0, devices)
-    def _(d):
-        add_rows(d, got_ref, d * width, slots)
-        guests = head[devices + d, LANES - 1]
+                add_pair(section, d, r0, rows_ref, d * width + r0, width, min(BATCH, width - r0))
+
+    for d in range(0, devices, 2):
+        add_rows(0, d, got_ref, width)
+        guests = jnp.maximum(head[devices + d, last], head[devices + d + 1, last])
         for r0 in range(guest_width - 8, -1, -8):
 
             @pl.when(guests > max(guest_width - 9 - r0, 0))
             def _():
-                add_group(devices + d, width - guest_width + r0, guest_ref, d * guest_width + r0, 8)
-
+                add_pair(1, d, width - guest_width + r0, guest_ref, d * guest_width + r0, guest_width, 8)
 
     if rounds == 2:
         more_width = more_ref.shape[0] // devices
 
-        @pl.loop(0, devices)
-        def _(d):
-            add_rows(2 * devices + d, more_ref, d * more_width, more_width)
+        @pl.loop(0, devices // 2)
+        def _(i):
+            add_rows(2, 2 * i, more_ref, more_width)
 
     groups = chunk // LANES
     stores = []
     for c in range(CHUNKS):
         heres = [pl.ds((c * groups + i) * LANES, LANES) for i in range(groups)]
         these = pl.ds(c * groups, groups)
-        squares = [jnp.transpose(jnp.square(sums[here, :])) for here in heres]
+        squares = [jnp.transpose(jnp.square(sums[0][here, :] + sums[1][here, :])) for here in heres]
         totals = jnp.concatenate([jnp.sum(x, axis=0, keepdims=True) for x in squares], axis=0)
         new_accum = accum_ref[these, :] + totals * (1.0 / LANES)
         accum_out[these, :] = new_accum
@@ -244,7 +254,7 @@
         loads[c].wait()
         for i, here in enumerate(heres):
             factor = jnp.transpose(jnp.broadcast_to(scale[i : i + 1, :], (LANES, LANES)))
-            table[here, :] = table[here, :] - factor * sums[here, :]
+            table[here, :] = table[here, :] - factor * (sums[0][here, :] + sums[1][here, :])
 
         store = pltpu.make_async_copy(
             table.at[pl.ds(c * chunk, chunk), :], table_out.at[pl.ds(c * chunk, chunk), :], sems_out.at[c]
@@ -264,7 +274,7 @@
     width = -(-capacity * 5 // 8 // 8) * 8
     guest_width = -(-width * 3 // 10 // 8) * 8
     slots = width - 1
-    more_slots = -(-(capacity - slots) // UNROLL) * UNROLL
+    more_slots = -(-(capacity - slots) // 16) * 16
     blocks = look_count // LANES
     vmem = pl.BlockSpec(memory_space=pltpu.VMEM)
     hbm = pl.BlockSpec(memory_space=pltpu.MemorySpace.HBM)
@@ -290,7 +300,11 @@
         ],
         compiler_params=pltpu.CompilerParams(vmem_limit_bytes=24 << 20),
         name="bin_rows",
-    )(row_ids.reshape(blocks, LANES), block_map.reshape(-1, LANES), grad_tiles)
+    )(
+        pltpu.with_memory_space_constraint(row_ids.reshape(blocks, LANES), pltpu.HBM),
+        pltpu.with_memory_space_constraint(block_map.reshape(-1, LANES), pltpu.HBM),
+        grad_tiles,
+    )
 
     got = lax.all_to_all(send, axes, split_axis=0, concat_axis=0, tiled=True)
     guests = got.reshape(devices, width, features)[:, width - guest_width :, :]
@@ -307,7 +321,7 @@
             in_specs=[vmem] * (2 * rounds + 1) + [hbm],
             out_specs=(hbm, vmem),
             scratch_shapes=[
-                pltpu.VMEM((rows_dev + 8, features), jnp.float32),
+                [pltpu.VMEM((rows_dev + 8, features), jnp.float32)] * 2,
                 pltpu.VMEM((rows_dev, features), jnp.float32),
                 pltpu.VMEM(((rounds + 1) * devices, LANES), jnp.int32),
                 pltpu.SMEM(((rounds + 1) * devices, LANES), jnp.int32),

time: 61.2 us -> 58.5 us (0.956)
  local copies, waits for them, and re-layouts: 1.42 us -> 0.03 us
  Pallas kernels: 16.4 us -> 15.2 us
    pallas_call x1, Pallas kernels: 9.94 us -> 8.48 us  [apply_step(): pl.pallas_call(functools.partial(update_kernel, devices, rounds), out_sha...]
    unnamed x6 -> x2, local copies, waits for them, and re-layouts: 1.39 us -> 0.01 us
where the time goes in v4:
time: 58.5 us; the launch traced here: 58.3 us
  blocking collectives  40.2 us (69%)
  Pallas kernels  15.2 us (26%)
  between operations  1.49 us (3%)
  other arithmetic  0.7 us (1%)
    all_to_all x1, blocking collectives, on_device(): got = lax.all_to_all(send, axes, split_axis=0, concat_axis=0, tiled=True)  40.2 us
    pallas_call x1, Pallas kernels, apply_step(): pl.pallas_call(functools.partial(update_kernel, devices, rounds), out_sha...  8.48 us
    pallas_call x1, Pallas kernels, on_device(): pl.pallas_call(functools.partial(bin_kernel, devices, lax.axis_size('gy')...  6.76 us
  transfers between devices with their start and end apart: 1, of which 1 were waited for; matrix products, arithmetic and copies ran while one was open for 1% of the time, Pallas kernels for 0%

profile of v4, /device:TPU:0, one launch (start us, length us, event | category | flops | bytes accessed | tf_op | source)
XLA Modules:
  0.0 58.3 jit_solution(7923771735898513251)
XLA Ops:
  0.6 0.0 copy-start
  0.6 6.8 %bin_rows.1 = (f32[2560,128]{1,0:T(8,128)S(1)}, s32[32,128]{1,0:T(8,128)S(1)}) custom-call(s32[16,128]{1,0:T(8,128)} %bitcast.43, s32[16,128]{1,0:T(8,128)} %bitcast.44, f32[2048,128]{1,0:T(8,128)} %grad_hbm.1), custom_call_target="tpu_custom_call" | custom-call | tf_op jit(solution)/shard_map/bin_rows/pallas_call | solution.py:282
  7.4 40.2 %all_to_all.27 = f32[32,80,128]{2,1,0:T(8,128)S(1)} all-to-all(f32[32,80,128]{2,1,0:T(8,128)S(1)} %bitcast.33), channel_id=1, replica_groups=mesh['gx'=4,'gy'=8] {'gx','gy'}, dimensions={0} | all-to-all | bytes 2621440 | tf_op jit(solution)/shard_map/all_to_all | solution.py:309
  47.7 0.1 collective-permute-start
  47.7 0.7 %slice_reduce_fusion = f32[]{:T(128)} fusion(f32[32,80,128]{2,1,0:T(8,128)S(1)} %all_to_all.27), kind=kLoop, calls=%fused_computation.31 | loop fusion | flops 31 | bytes 132 | tf_op jit(solution)/shard_map/reduce_max | solution.py:358
  49.1 0.4 collective-permute-done
  49.4 0.0 copy-done
  49.4 8.7 %conditional.1 = (f32[8192,128]{1,0:T(8,128)}, f32[8192]{0:T(1024)}) conditional(s32[]{:T(128)} %convert_element_type.9, (f32[8192]{0:T(1024)S(1)}, f32[2560,128]{1,0:T(8,128)S(1)}, f32[768,128]{1,0:T(8,128)S(1)}, f32[8192,128]{1,0:T(8,128)}) %tuple.27, (s32[32,128]{1,0:T(8,128)S(1)}, f32[2048,128]{1,0:T(8,128)}, f32[8192]{0:T(1024)S(1)}, ...), branch_computations={%region_1.0_spmd, %region_2.8_spmd} | conditional | flops 46505952 | bytes 4453460 | solution.py:359
  49.5 8.5 %apply_step_1.1 = (f32[8192,128]{1,0:T(8,128)}, f32[64,128]{1,0:T(8,128)}) custom-call(f32[2560,128]{1,0:T(8,128)S(1)} %get-tuple-element.20.refs_0_, f32[768,128]{1,0:T(8,128)S(1)} %get-tuple-element.21.refs_1_, f32[64,128]{1,0:T(8,128)S(1)} %bitcast.40, f32[8192,128]{1,0:T(8,128)} %get-tuple-element.23.refs_3_), custom_call_target="tpu_custom_call" | custom-call | tf_op jit(solution)/shard_map/cond/branch_0_fun/apply_step_1/pallas_call | solution.py:315
  (1 shorter events, 0.0 us)
Async XLA Ops:
  0.6 48.8 %copy-start = (f32[8192]{0:T(1024)S(1)}, f32[8192]{0:T(1024)}, u32[]{:S(2)}) copy-start(f32[8192]{0:T(1024)} %param.11) | copy-start | bytes 98308
  47.7 1.8 %collective-permute-start = (f32[32,24,128]{2,1,0:T(8,128)S(1)}, f32[32,24,128]{2,1,0:T(8,128)S(1)}, u32[]{:S(2)}, u32[]{:S(2)}) collective-permute-start(f32[32,24,128]{2,1,0:T(8,128)S(1)} %slice.15), channel_id=1, source_target_pairs={{0,8},{8,0},{16,24},{24,16},{1,9},{9,1},{17,25},{25,17},{2,10},{10... | collective-permute-start | bytes 1179656 | tf_op jit(solution)/shard_map/ppermute | solution.py:311

commit v5 on v4

--- a/solution.py
+++ b/solution.py
@@ -12,7 +12,7 @@
 STREAMS = 8
 GROUP = 8
 BATCH = 16
-CHUNKS = 8
+CHUNKS = 4
 
 learning_rate = 0.25
 epsilon = 1e-08
@@ -242,7 +242,7 @@
             add_rows(2, 2 * i, more_ref, more_width)
 
     groups = chunk // LANES
-    stores = []
+    scales = []
     for c in range(CHUNKS):
         heres = [pl.ds((c * groups + i) * LANES, LANES) for i in range(groups)]
         these = pl.ds(c * groups, groups)
@@ -250,10 +250,14 @@
         totals = jnp.concatenate([jnp.sum(x, axis=0, keepdims=True) for x in squares], axis=0)
         new_accum = accum_ref[these, :] + totals * (1.0 / LANES)
         accum_out[these, :] = new_accum
-        scale = learning_rate / (jnp.sqrt(new_accum) + epsilon)
+        scales.append(learning_rate / (jnp.sqrt(new_accum) + epsilon))
+
+    stores = []
+    for c in range(CHUNKS):
         loads[c].wait()
-        for i, here in enumerate(heres):
-            factor = jnp.transpose(jnp.broadcast_to(scale[i : i + 1, :], (LANES, LANES)))
+        for i in range(groups):
+            here = pl.ds((c * groups + i) * LANES, LANES)
+            factor = jnp.transpose(jnp.broadcast_to(scales[c][i : i + 1, :], (LANES, LANES)))
             table[here, :] = table[here, :] - factor * (sums[0][here, :] + sums[1][here, :])
 
         store = pltpu.make_async_copy(

time: 58.5 us -> 58.2 us (level)
  no operation moved by 1% of the time
where the time goes in v5:
time: 58.2 us; the launch traced here: 58.1 us
  blocking collectives  40.2 us (69%)
  Pallas kernels  15 us (26%)
  between operations  1.49 us (3%)
  other arithmetic  0.7 us (1%)
    all_to_all x1, blocking collectives, on_device(): got = lax.all_to_all(send, axes, split_axis=0, concat_axis=0, tiled=True)  40.2 us
    pallas_call x1, Pallas kernels, apply_step(): pl.pallas_call(functools.partial(update_kernel, devices, rounds), out_sha...  8.23 us
    pallas_call x1, Pallas kernels, on_device(): pl.pallas_call(functools.partial(bin_kernel, devices, lax.axis_size('gy')...  6.76 us
  transfers between devices with their start and end apart: 1, of which 1 were waited for; matrix products, arithmetic and copies ran while one was open for 1% of the time, Pallas kernels for 0%

profile of v5, /device:TPU:0, one launch (start us, length us, event | category | flops | bytes accessed | tf_op | source)
XLA Modules:
  0.0 58.1 jit_solution(13936280677303585880)
XLA Ops:
  0.6 0.0 copy-start
  0.6 6.8 %bin_rows.1 = (f32[2560,128]{1,0:T(8,128)S(1)}, s32[32,128]{1,0:T(8,128)S(1)}) custom-call(s32[16,128]{1,0:T(8,128)} %bitcast.43, s32[16,128]{1,0:T(8,128)} %bitcast.44, f32[2048,128]{1,0:T(8,128)} %grad_hbm.1), custom_call_target="tpu_custom_call" | custom-call | tf_op jit(solution)/shard_map/bin_rows/pallas_call | solution.py:286
  7.4 40.2 %all_to_all.27 = f32[32,80,128]{2,1,0:T(8,128)S(1)} all-to-all(f32[32,80,128]{2,1,0:T(8,128)S(1)} %bitcast.33), channel_id=1, replica_groups=mesh['gx'=4,'gy'=8] {'gx','gy'}, dimensions={0} | all-to-all | bytes 2621440 | tf_op jit(solution)/shard_map/all_to_all | solution.py:313
  47.7 0.1 collective-permute-start
  47.7 0.7 %slice_reduce_fusion = f32[]{:T(128)} fusion(f32[32,80,128]{2,1,0:T(8,128)S(1)} %all_to_all.27), kind=kLoop, calls=%fused_computation.31 | loop fusion | flops 31 | bytes 132 | tf_op jit(solution)/shard_map/reduce_max | solution.py:362
  49.1 0.4 collective-permute-done
  49.4 0.0 copy-done
  49.4 8.5 %conditional.1 = (f32[8192,128]{1,0:T(8,128)}, f32[8192]{0:T(1024)}) conditional(s32[]{:T(128)} %convert_element_type.9, (f32[8192]{0:T(1024)S(1)}, f32[2560,128]{1,0:T(8,128)S(1)}, f32[768,128]{1,0:T(8,128)S(1)}, f32[8192,128]{1,0:T(8,128)}) %tuple.27, (s32[32,128]{1,0:T(8,128)S(1)}, f32[2048,128]{1,0:T(8,128)}, f32[8192]{0:T(1024)S(1)}, ...), branch_computations={%region_1.0_spmd, %region_2.8_spmd} | conditional | flops 46505952 | bytes 4453460 | solution.py:363
  49.4 8.2 %apply_step_1.1 = (f32[8192,128]{1,0:T(8,128)}, f32[64,128]{1,0:T(8,128)}) custom-call(f32[2560,128]{1,0:T(8,128)S(1)} %get-tuple-element.20.refs_0_, f32[768,128]{1,0:T(8,128)S(1)} %get-tuple-element.21.refs_1_, f32[64,128]{1,0:T(8,128)S(1)} %bitcast.40, f32[8192,128]{1,0:T(8,128)} %get-tuple-element.23.refs_3_), custom_call_target="tpu_custom_call" | custom-call | tf_op jit(solution)/shard_map/cond/branch_0_fun/apply_step_1/pallas_call | solution.py:319
  (1 shorter events, 0.0 us)
Async XLA Ops:
  0.6 48.8 %copy-start = (f32[8192]{0:T(1024)S(1)}, f32[8192]{0:T(1024)}, u32[]{:S(2)}) copy-start(f32[8192]{0:T(1024)} %param.11) | copy-start | bytes 98308
  47.7 1.8 %collective-permute-start = (f32[32,24,128]{2,1,0:T(8,128)S(1)}, f32[32,24,128]{2,1,0:T(8,128)S(1)}, u32[]{:S(2)}, u32[]{:S(2)}) collective-permute-start(f32[32,24,128]{2,1,0:T(8,128)S(1)} %slice.15), channel_id=1, source_target_pairs={{0,8},{8,0},{16,24},{24,16},{1,9},{9,1},{17,25},{25,17},{2,10},{10... | collective-permute-start | bytes 1179656 | tf_op jit(solution)/shard_map/ppermute | solution.py:315
